TPU v7x, 512 devices: a whole 4x8x8 slice. The times are simulated.
512 devices in a mesh: seq: 64 (over z, y), fsdp: 8 (over x, core).
Axes of the slice: x: 4, y: 8, z: 8, core: 2. Of those that a mesh axis runs over, the one named last changes fastest.
Arguments:
- query: bfloat16 [32768, 4096], P('seq', 'fsdp'), may hold values from -6 to 6
- key: bfloat16 [32768, 4096], P('seq', 'fsdp'), may hold values from -6 to 6
- value: bfloat16 [32768, 4096], P('seq', 'fsdp'), may hold values from -16 to 16, as said below
- cotangent: bfloat16 [32768, 4096], P('seq', 'fsdp'), may hold values from -16 to 16
- gain: float32 [4096], P('fsdp'), may hold values from 0.1 to 1.9
Outputs:
- query_grad: bfloat16 [32768, 4096], P('seq', 'fsdp')
- key_grad: bfloat16 [32768, 4096], P('seq', 'fsdp')
- value_grad: bfloat16 [32768, 4096], P('seq', 'fsdp')
- gain_grad: float32 [4096], P('fsdp')
Inputs may be any that keep to these rules, and one draw needn't show every extreme that they name: `value`: values whose typical size differs from head to head.
All inputs are finite; a program needn't handle non-finite values.
Results may differ from a plain program's by a relative error of at most 0.0057.
Values sent between devices are 32-bit elements; how exact they have to be, the bound alone decides.
No kernel may reach another device: no remote copies, remote signals or barrier semaphores. Data moves between devices by JAX's collectives and lax.ppermute only.
A program may use at most 64 MiB of HBM per device.

v0:
```python
import math

import jax
import jax.numpy as jnp
from jax import lax
from jax.sharding import PartitionSpec as P

HEAD_DIM = 128
HD = 4096


def prefix_2(part, axis, combine, identity, reverse):
    count = lax.axis_size(axis)
    place = lax.axis_index(axis)
    ahead = count - 1 - place if reverse else place
    gathered = lax.all_gather(part, axis)
    state = jnp.zeros_like(part) + jnp.asarray(identity, part.dtype)

    def one(turn, state):
        source = count - 1 - turn if reverse else turn
        return combine(state, lax.dynamic_index_in_dim(gathered, source, 0, False))

    return lax.fori_loop(0, ahead, one, state)


def add_states(earlier, later):
    return earlier + later


def shards(query, key, value, cotangent, gain):
    rows = query.shape[0]
    width = query.shape[1]
    heads = width // HEAD_DIM
    shape = (rows, heads, HEAD_DIM)
    queries = query.reshape(shape)
    keys = key.reshape(shape)
    values = value.reshape(shape)
    causal = jnp.tril(jnp.ones((rows, rows), dtype=bool))
    own_state = jnp.einsum("tha,thb->hab", keys, values, preferred_element_type=jnp.float32)
    prefix = prefix_2(own_state, "seq", add_states, jnp.zeros_like(own_state), False)
    prefix_low = prefix.astype(jnp.bfloat16)
    scores = jnp.einsum("tha,sha->hts", queries, keys, preferred_element_type=jnp.float32)
    weights = jnp.where(causal[None], scores, 0.0).astype(jnp.bfloat16)
    attended = jnp.einsum("hts,shb->thb", weights, values, preferred_element_type=jnp.float32)
    attended = attended + jnp.einsum(
        "tha,hab->thb", queries, prefix_low, preferred_element_type=jnp.float32
    )
    attended = attended.reshape(rows, width)
    squares = lax.psum(jnp.sum(attended * attended, axis=-1), "fsdp")
    inv_rms = lax.rsqrt(squares / HD + 1e-05)[:, None]
    normed = attended * inv_rms
    upstream = cotangent.astype(jnp.float32)
    partial_gain = jnp.sum(upstream * normed, axis=0)
    scaled = upstream * gain
    crossed = lax.psum(jnp.sum(scaled * normed, axis=-1), "fsdp")
    attended_grad = (scaled - normed * (crossed / HD)[:, None]) * inv_rms
    grads = attended_grad.astype(jnp.bfloat16).reshape(shape)
    own_grad = jnp.einsum("tha,thb->hab", queries, grads, preferred_element_type=jnp.float32)
    suffix = prefix_2(own_grad, "seq", add_states, jnp.zeros_like(own_grad), True)
    suffix_low = suffix.astype(jnp.bfloat16)
    score_grad = jnp.einsum("thb,shb->hts", grads, values, preferred_element_type=jnp.float32)
    score_grad = jnp.where(causal[None], score_grad, 0.0).astype(jnp.bfloat16)
    query_grad = jnp.einsum("hts,sha->tha", score_grad, keys, preferred_element_type=jnp.float32)
    query_grad = query_grad + jnp.einsum(
        "thb,hab->tha", grads, prefix_low, preferred_element_type=jnp.float32
    )
    key_grad = jnp.einsum("hts,tha->sha", score_grad, queries, preferred_element_type=jnp.float32)
    key_grad = key_grad + jnp.einsum(
        "shb,hab->sha", values, suffix_low, preferred_element_type=jnp.float32
    )
    value_grad = jnp.einsum("hts,thb->shb", weights, grads, preferred_element_type=jnp.float32)
    value_grad = value_grad + jnp.einsum(
        "sha,hab->shb", keys, suffix_low, preferred_element_type=jnp.float32
    )
    factor = 1.0 / math.sqrt(rows * lax.axis_size("seq"))
    total_gain = lax.psum(partial_gain, "seq")
    out_shape = (rows, width)
    return (
        query_grad.reshape(out_shape).astype(jnp.bfloat16),
        key_grad.reshape(out_shape).astype(jnp.bfloat16),
        value_grad.reshape(out_shape).astype(jnp.bfloat16),
        total_gain * factor,
    )


def solution(mesh):
    in_specs = (P("seq", "fsdp"), P("seq", "fsdp"), P("seq", "fsdp"), P("seq", "fsdp"), P("fsdp"))
    out_specs = (P("seq", "fsdp"), P("seq", "fsdp"), P("seq", "fsdp"), P("fsdp"))
    return jax.shard_map(shards, mesh=mesh, in_specs=in_specs, out_specs=out_specs, check_vma=False)
```

profile of v0, /device:TPU:2, one launch (start us, length us, event | category | flops | bytes accessed | tf_op | source)
XLA Modules:
  0.0 482.6 jit_solution(4760123560782136005)
XLA Ops:
  7.2 1.3 copy.101
  8.6 2.0 fusion.15
  12.3 1.3 copy-done.1
  14.4 141.6 %all-gather.5.cloned.1.call-done = f32[256,128,128]{2,1,0:T(8,128)} async-done(((f32[4,128,128]{2,1,0:T(8,128)}), f32[256,128,128]{2,1,0:T(8,128)}) %all-gather.5.cloned.1.call-update) | async-done | bytes 16777232 | tf_op jit(solution)/shard_map/all_gather | solution.py:16
  156.1 1.3 multiply_reduce_fusion
  157.4 11.4 %psum.21 = f32[512]{0:T(512)S(1)} all-reduce(f32[512]{0:T(512)S(1)} %get-tuple-element.115), channel_id=1, replica_groups=mesh['seq'=64,'fsdp'=8] {'fsdp'}, use_global_device_ids=true, to_apply=%region_3.4 | all-reduce | flops 512 | bytes 4096 | tf_op jit(solution)/shard_map/psum | solution.py:49
  168.9 1.6 copy.39
  170.9 12.4 %psum.22 = f32[512]{0:T(512)S(1)} all-reduce(f32[512]{0:T(512)S(1)} %get-tuple-element.98), channel_id=1, replica_groups=mesh['seq'=64,'fsdp'=8] {'fsdp'}, use_global_device_ids=true, to_apply=%region_5.6 | all-reduce | flops 512 | bytes 4096 | tf_op jit(solution)/shard_map/psum | solution.py:55
  183.3 1.1 fusion.10
  184.4 1.3 copy.57
  188.5 1.1 fusion.3
  189.6 2.0 copy.52
  191.7 210.7 %psum.23 = f32[512]{0:T(512)S(1)} all-reduce(f32[512]{0:T(512)S(1)} %get-tuple-element.97), channel_id=1, replica_groups=mesh['seq'=64,'fsdp'=8] {'seq'}, use_global_device_ids=true, to_apply=%region_9.10 | all-reduce | flops 512 | bytes 4096 | tf_op jit(solution)/shard_map/psum | solution.py:76
  402.9 1.4 fusion.37
  404.9 65.2 %while.23 = (s32[]{:T(128)}, f32[4,128,128]{2,1,0:T(8,128)S(1)}, s32[]{:T(128)}, f32[64,4,128,128]{3,2,1,0:T(8,128)}, s32[]{:T(128)}, /*index=5*/s32[]{:T(128)}, s32[]{:T(128)}, s32[]{:T(128)}) while((s32[]{:T(128)}, f32[4,128,128]{2,1,0:T(8,128)S(1)}, s32[]{:T(128)}, f32[64,4,128,128]{3,2,1,0:T(8,128)}, s32[]{:T(128)}, /*index=5*/s32[]{:T(128)}, ...), condition=%wide.region_7.8_spmd, body=%wide.region_6.7_spmd.sunk | while | flops 65542 | bytes 786575 | solution.py:23
  404.9 1.1 bitcast_add_fusion.5
  407.1 1.0 bitcast_add_fusion.5
  408.1 1.0 bitcast_add_fusion.5
  409.1 1.0 bitcast_add_fusion.5
  417.4 1.0 bitcast_add_fusion.5
  418.4 1.0 bitcast_add_fusion.5
  419.5 1.0 bitcast_add_fusion.5
  470.1 2.2 fusion.5
  472.4 2.0 copy.54
  (103 shorter events, 64.8 us)
Async XLA Ops:
  7.2 4.3 copy-start
  7.2 4.3 copy-start.9
  7.2 148.8 %all-gather.5.cloned.1.call-start = ((), (), s32[]{:S(2)}) async-start(), calls=%async_computation | async-start | bytes 17039360 | tf_op jit(solution)/shard_map/all_gather | solution.py:16
  10.6 394.2 %all-gather.7.cloned.1.call-start = ((), (), s32[]{:S(2)}) async-start(), calls=%async_computation.1 | async-start | bytes 17039360 | tf_op jit(solution)/shard_map/all_gather | solution.py:16
  10.8 0.7 copy-start.10
  11.5 2.1 copy-start.5
  12.2 1.3 copy-start.1
  156.1 14.4 %copy-start.8 = (bf16[512,512]{1,0:T(8,128)(2,1)S(1)}, bf16[512,512]{1,0:T(8,128)(2,1)}, u32[]{:S(2)}) copy-start(bf16[512,512]{1,0:T(8,128)(2,1)} %param.12) | copy-start | bytes 1572868
  156.1 14.4 %copy-start.12 = (f32[512]{0:T(512)S(1)}, f32[512]{0:T(512)}, u32[]{:S(2)}) copy-start(f32[512]{0:T(512)} %param.13) | copy-start | bytes 6148
  184.4 2.5 copy-start.11
  187.7 1.9 copy-start.3
  188.5 214.4 %copy-start.2 = (bf16[4,512,512]{2,1,0:T(8,128)(2,1)S(1)}, bf16[4,512,512]{2,1,0:T(8,128)(2,1)}, u32[]{:S(2)}) copy-start(bf16[4,512,512]{2,1,0:T(8,128)(2,1)} %copy-done.1) | copy-start | bytes 6291460
  402.3 2.0 copy-start.4
  404.9 65.2 %copy-start.7 = (f32[4,128,512]{2,1,0:T(8,128)S(1)}, f32[4,128,512]{2,1,0:T(8,128)}, u32[]{:S(2)}) copy-start(f32[4,128,512]{2,1,0:T(8,128)} %fusion.37) | copy-start | bytes 3145732
  470.1 4.3 copy-start.6
Sparse Core Ops, SparseCore 0:
  11.6 144.3 all-gather.4
  187.0 201.0 all-gather.6
where the time goes:
time: 485 us; the launch traced here: 483 us
  blocking collectives  235 us (48%)
  waiting for transfers between devices  142 us (29%)
  other arithmetic  65.9 us (14%)
  between operations  14.3 us (3%)
  matrix products  12.4 us (3%)
  local copies, waits for them, and re-layouts  12.2 us (3%)
    psum x1, blocking collectives, shards(): total_gain = lax.psum(partial_gain, 'seq')  211 us
    all_gather x2, waiting for transfers between devices, prefix_2(): gathered = lax.all_gather(part, axis)  142 us
    add x63, other arithmetic, add_states(): return earlier + later  63.7 us
    psum x1, blocking collectives, shards(): crossed = lax.psum(jnp.sum(scaled * normed, axis=-1), 'fsdp')  12.4 us
    psum x1, blocking collectives, shards(): squares = lax.psum(jnp.sum(attended * attended, axis=-1), 'fsdp')  11.4 us
  transfers between devices with their start and end apart: 2, of which 1 were waited for; matrix products, arithmetic and copies ran while one was open for 2% of the time, Pallas kernels for 0%

commit v1 on v0

v1 whole, which is shorter than its diff:
```python
import math

import jax
import jax.numpy as jnp
from jax import lax
from jax.experimental import pallas as pl
from jax.experimental.pallas import tpu as pltpu
from jax.sharding import PartitionSpec as P

HEAD_DIM = 128
HD = 4096
EPS = 1e-05
F32 = jnp.float32
BF16 = jnp.bfloat16
ROWS = 8
GAIN_ROWS = ROWS + 1


def dot(a, b, over_a, over_b):
    return lax.dot_general(a, b, (((over_a,), (over_b,)), ((), ())), preferred_element_type=F32)


def cols(h):
    return pl.ds(h * HEAD_DIM, HEAD_DIM)


def call(kernel, outs, flops, *args):
    out_bytes = sum(math.prod(o.shape) * o.dtype.itemsize for o in outs)
    in_bytes = sum(math.prod(a.shape) * a.dtype.itemsize for a in args)
    return pl.pallas_call(
        kernel,
        out_shape=tuple(outs),
        in_specs=[pl.BlockSpec(memory_space=pltpu.VMEM)] * len(args),
        out_specs=tuple(pl.BlockSpec(memory_space=pltpu.VMEM) for _ in outs),
        cost_estimate=pl.CostEstimate(
            flops=flops, transcendentals=0, bytes_accessed=in_bytes + out_bytes
        ),
        name=kernel.__name__,
    )(*args)


def state_kernel(k_ref, v_ref, out_ref):
    for h in range(k_ref.shape[1] // HEAD_DIM):
        out_ref[pl.ds(h * HEAD_DIM, HEAD_DIM), :] = dot(k_ref[:, cols(h)], v_ref[:, cols(h)], 0, 0)


def masked(scores, first_row, first_col):
    row = lax.broadcasted_iota(jnp.int32, scores.shape, 0) + first_row
    col = lax.broadcasted_iota(jnp.int32, scores.shape, 1) + first_col
    return jnp.where(row >= col, scores, 0.0)


def local_kernel(q_ref, k_ref, v_ref, weights_ref, local_ref):
    rows = q_ref.shape[0]
    block = min(256, rows)
    for h in range(q_ref.shape[1] // HEAD_DIM):
        for i in range(rows // block):
            mine = pl.ds(i * block, block)
            ends = (i + 1) * block
            scores = dot(q_ref[mine, cols(h)], k_ref[:ends, cols(h)], 1, 1)
            weights = masked(scores, i * block, 0).astype(BF16)
            weights_ref[h, mine, :ends] = weights
            local_ref[mine, cols(h)] = dot(weights, v_ref[:ends, cols(h)], 1, 0)


def prefix_kernel(in_ref, out_ref):
    acc = jnp.zeros(in_ref.shape[1:], F32)
    for j in range(in_ref.shape[0]):
        out_ref[j] = acc
        acc = acc + in_ref[j]


def suffix_kernel(in_ref, out_ref):
    count = in_ref.shape[0] // GAIN_ROWS
    acc = jnp.zeros((ROWS, HEAD_DIM), F32)
    gain = jnp.zeros((1, HEAD_DIM), F32)
    for j in reversed(range(count)):
        out_ref[pl.ds(j * GAIN_ROWS, ROWS), :] = acc
        acc = acc + in_ref[pl.ds(j * GAIN_ROWS, ROWS), :]
        gain = gain + in_ref[pl.ds(j * GAIN_ROWS + ROWS, 1), :]
    for j in range(count):
        out_ref[pl.ds(j * GAIN_ROWS + ROWS, 1), :] = gain


def stats_kernel(q_ref, local_ref, prefix_ref, cot_ref, gain_ref, att_ref, low_ref, out_ref):
    rows, width = q_ref.shape
    squares = jnp.zeros((rows, HEAD_DIM), F32)
    crossed = jnp.zeros((rows, HEAD_DIM), F32)
    for h in range(width // HEAD_DIM):
        low = prefix_ref[pl.ds(h * HEAD_DIM, HEAD_DIM), :].astype(BF16)
        low_ref[pl.ds(h * HEAD_DIM, HEAD_DIM), :] = low
        att = local_ref[:, cols(h)] + dot(q_ref[:, cols(h)], low, 1, 0)
        att_ref[:, cols(h)] = att
        squares = squares + att * att
        crossed = crossed + att * (cot_ref[:, cols(h)].astype(F32) * gain_ref[:, cols(h)])
    parts = rows // HEAD_DIM
    peers = out_ref.shape[0]
    for n, sums in enumerate((squares, crossed)):
        for i in range(parts):
            turned = sums[i * HEAD_DIM : (i + 1) * HEAD_DIM, :].T
            line = jnp.sum(turned, axis=0, keepdims=True)
            for peer in range(peers):
                out_ref[peer, pl.ds(n * parts + i, 1), :] = line


def grads_kernel(att_ref, cot_ref, gain_ref, stats_ref, q_ref, grads_ref, out_ref):
    rows, width = att_ref.shape
    parts = rows // HEAD_DIM
    heads = width // HEAD_DIM
    stats = jnp.sum(stats_ref[...], axis=0)
    inv = lax.rsqrt(stats[:parts] / HD + EPS)
    mean = stats[parts:] * inv / HD
    for i in range(parts):
        mine = pl.ds(i * HEAD_DIM, HEAD_DIM)
        square = (HEAD_DIM, HEAD_DIM)
        inv_i = jnp.broadcast_to(inv[i : i + 1, :], square).T
        mean_i = jnp.broadcast_to(mean[i : i + 1, :], square).T
        for h in range(heads):
            normed = att_ref[mine, cols(h)] * inv_i
            upstream = cot_ref[mine, cols(h)].astype(F32)
            scaled = upstream * gain_ref[:, cols(h)]
            grads_ref[mine, cols(h)] = ((scaled - normed * mean_i) * inv_i).astype(BF16)
            line = jnp.sum(upstream * normed, axis=0, keepdims=True)
            at = pl.ds(h * GAIN_ROWS + ROWS, 1)
            if i == 0:
                out_ref[at, :] = line
            else:
                out_ref[at, :] = out_ref[at, :] + line
    slices = HEAD_DIM // ROWS
    for h in range(heads):
        state = dot(q_ref[:, cols(h)], grads_ref[:, cols(h)], 0, 0)
        for s in range(slices):
            piece = h * slices + s
            out_ref[pl.ds(piece * GAIN_ROWS, ROWS), :] = state[s * ROWS : (s + 1) * ROWS, :]
            if piece >= heads:
                out_ref[pl.ds(piece * GAIN_ROWS + ROWS, 1), :] = jnp.zeros((1, HEAD_DIM), F32)


def backward_kernel(
    q_ref, k_ref, v_ref, grads_ref, weights_ref, low_ref, query_ref, key_ref, value_ref, score_ref
):
    rows = q_ref.shape[0]
    block = min(256, rows)
    for h in range(q_ref.shape[1] // HEAD_DIM):
        low = low_ref[pl.ds(h * HEAD_DIM, HEAD_DIM), :]
        for i in range(rows // block):
            mine = pl.ds(i * block, block)
            ends = (i + 1) * block
            scores = dot(grads_ref[mine, cols(h)], v_ref[:ends, cols(h)], 1, 1)
            score = masked(scores, i * block, 0).astype(BF16)
            score_ref[mine, :ends] = score
            query = dot(score, k_ref[:ends, cols(h)], 1, 0)
            query = query + dot(grads_ref[mine, cols(h)], low, 1, 1)
            query_ref[mine, cols(h)] = query.astype(BF16)
        for i in range(rows // block):
            mine = pl.ds(i * block, block)
            first = i * block
            key_ref[mine, cols(h)] = dot(score_ref[first:, mine], q_ref[first:, cols(h)], 0, 0)
            value_ref[mine, cols(h)] = dot(
                weights_ref[h, first:, mine], grads_ref[first:, cols(h)], 0, 0
            )


def final_kernel(key_ref, value_ref, k_ref, v_ref, suffix_ref, key_out, value_out, gain_out):
    heads = k_ref.shape[1] // HEAD_DIM
    slices = HEAD_DIM // ROWS
    length = suffix_ref.shape[0] // GAIN_ROWS * k_ref.shape[0]
    for h in range(heads):
        pieces = [
            suffix_ref[pl.ds((h * slices + s) * GAIN_ROWS, ROWS), :] for s in range(slices)
        ]
        low = jnp.concatenate(pieces, axis=0).astype(BF16)
        key = key_ref[:, cols(h)] + dot(v_ref[:, cols(h)], low, 1, 1)
        key_out[:, cols(h)] = key.astype(BF16)
        value = value_ref[:, cols(h)] + dot(k_ref[:, cols(h)], low, 1, 0)
        value_out[:, cols(h)] = value.astype(BF16)
        line = suffix_ref[pl.ds(h * GAIN_ROWS + ROWS, 1), :]
        gain_out[pl.ds(h, 1), :] = line * (1.0 / math.sqrt(length))


def exchange(x, axis, shape):
    count = lax.axis_size(axis)
    moved = lax.all_to_all(x.reshape((count,) + shape), axis, 0, 0, tiled=True)
    return moved.reshape(x.shape)


def shards(query, key, value, cotangent, gain):
    rows, width = query.shape
    heads = width // HEAD_DIM
    blocks = lax.axis_size("seq")
    peers = lax.axis_size("fsdp")
    sds = jax.ShapeDtypeStruct
    gain_row = gain.reshape(1, width)
    small = 2 * rows * width * HEAD_DIM
    big = 2 * rows * rows * width

    (state,) = call(state_kernel, [sds((width, HEAD_DIM), F32)], small, key, value)
    slices = exchange(state, "seq", (ROWS, HEAD_DIM))
    weights, local = call(
        local_kernel,
        [sds((heads, rows, rows), BF16), sds((rows, width), F32)],
        2 * big,
        query,
        key,
        value,
    )
    slices = slices.reshape(blocks, ROWS, HEAD_DIM)
    (slices,) = call(prefix_kernel, [sds(slices.shape, F32)], width * HEAD_DIM, slices)
    prefix = exchange(slices.reshape(width, HEAD_DIM), "seq", (ROWS, HEAD_DIM))

    attended, prefix_low, stats = call(
        stats_kernel,
        [
            sds((rows, width), F32),
            sds((width, HEAD_DIM), BF16),
            sds((peers, 2 * rows // HEAD_DIM, HEAD_DIM), F32),
        ],
        small,
        query,
        local,
        prefix,
        cotangent,
        gain_row,
    )
    stats = lax.all_to_all(stats, "fsdp", 0, 0, tiled=True)
    grads, grad_state = call(
        grads_kernel,
        [sds((rows, width), BF16), sds((blocks * GAIN_ROWS, HEAD_DIM), F32)],
        small,
        attended,
        cotangent,
        gain_row,
        stats,
        query,
    )
    grad_slices = exchange(grad_state, "seq", (GAIN_ROWS, 1, HEAD_DIM))
    query_grad, key_local, value_local, _ = call(
        backward_kernel,
        [
            sds((rows, width), BF16),
            sds((rows, width), F32),
            sds((rows, width), F32),
            sds((rows, rows), BF16),
        ],
        4 * big + small,
        query,
        key,
        value,
        grads,
        weights,
        prefix_low,
    )
    (grad_slices,) = call(
        suffix_kernel, [sds(grad_slices.shape, F32)], width * HEAD_DIM, grad_slices
    )
    suffix = exchange(grad_slices, "seq", (GAIN_ROWS, 1, HEAD_DIM))
    key_grad, value_grad, gain_grad = call(
        final_kernel,
        [
            sds((rows, width), BF16),
            sds((rows, width), BF16),
            sds((heads, HEAD_DIM), F32),
        ],
        2 * small,
        key_local,
        value_local,
        key,
        value,
        suffix,
    )
    return query_grad, key_grad, value_grad, gain_grad.reshape(width)


def solution(mesh):
    in_specs = (P("seq", "fsdp"), P("seq", "fsdp"), P("seq", "fsdp"), P("seq", "fsdp"), P("fsdp"))
    out_specs = (P("seq", "fsdp"), P("seq", "fsdp"), P("seq", "fsdp"), P("fsdp"))
    return jax.shard_map(shards, mesh=mesh, in_specs=in_specs, out_specs=out_specs, check_vma=False)
```

time: 485 us -> 117 us (0.24)
  the two profiles are of different devices: /device:TPU:2 before, /device:TPU:8 now
where the time goes in v1:
time: 117 us
  blocking collectives  62 us (53%)
  Pallas kernels  25.1 us (21%)
  waiting for transfers between devices  17.4 us (15%)
  starting transfers between devices  10.2 us (9%)
  local copies, waits for them, and re-layouts  1.41 us (1%)
    all_to_all x2, blocking collectives, exchange(): moved = lax.all_to_all(x.reshape((count,) + shape), axis, 0, 0, tiled=True)  52.2 us
    pallas_call x8, Pallas kernels, call(): pl.pallas_call(kernel, out_shape=tuple(outs), in_specs=[pl.BlockSpec(memo...  25.1 us
    all_to_all x2, waiting for transfers between devices, exchange(): moved = lax.all_to_all(x.reshape((count,) + shape), axis, 0, 0, tiled=True)  17.4 us
    all_to_all x2, starting transfers between devices, exchange(): moved = lax.all_to_all(x.reshape((count,) + shape), axis, 0, 0, tiled=True)  10.2 us
    all_to_all x1, blocking collectives, shards(): stats = lax.all_to_all(stats, 'fsdp', 0, 0, tiled=True)  9.84 us
  transfers between devices with their start and end apart: 2, of which 2 were waited for; matrix products, arithmetic and copies ran while one was open for 0% of the time, Pallas kernels for 9%

profile of v1, /device:TPU:8, one launch (start us, length us, event | category | flops | bytes accessed | tf_op | source)
XLA Modules:
  0.0 116.8 jit_solution(7688992429105095408)
XLA Ops:
  0.6 2.3 %state_kernel.1 = f32[512,128]{1,0:T(8,128)} custom-call(bf16[512,512]{1,0:T(8,128)(2,1)} %k_ref.7, bf16[512,512]{1,0:T(8,128)(2,1)} %v_ref.7), custom_call_target="tpu_custom_call" | custom-call | flops 67108864 | bytes 1310720 | tf_op jit(solution)/shard_map/state_kernel/pallas_call | solution.py:30
  2.9 31.0 %all_to_all.25.in_ref = f32[64,8,128]{2,1,0:T(8,128)} all-to-all(f32[64,8,128]{2,1,0:T(8,128)} %bitcast.11), channel_id=1, replica_groups=mesh['seq'=64,'fsdp'=8] {'seq'}, dimensions={0} | all-to-all | bytes 524288 | tf_op jit(solution)/shard_map/all_to_all | solution.py:183
  33.9 1.7 %prefix_kernel.1 = f32[64,8,128]{2,1,0:T(8,128)} custom-call(f32[64,8,128]{2,1,0:T(8,128)} %all_to_all.25.in_ref), custom_call_target="tpu_custom_call" | custom-call | flops 65536 | bytes 524288 | tf_op jit(solution)/shard_map/prefix_kernel/pallas_call | solution.py:30
  35.6 5.1 %all-to-all-start.1 = ((f32[64,8,128]{2,1,0:T(8,128)}), f32[64,8,128]{2,1,0:T(8,128)S(1)}, u32[]{:S(2)}, u32[]{:S(2)}) async-start(f32[64,8,128]{2,1,0:T(8,128)} %prefix_kernel.1), calls=%async_computation.1 | async-start | bytes 524288 | tf_op jit(solution)/shard_map/all_to_all | solution.py:183
  40.7 4.3 %local_kernel.1 = (bf16[4,512,512]{2,1,0:T(8,128)(2,1)}, f32[512,512]{1,0:T(8,128)}) custom-call(bf16[512,512]{1,0:T(8,128)(2,1)} %q_ref.7, bf16[512,512]{1,0:T(8,128)(2,1)} %k_ref.7, bf16[512,512]{1,0:T(8,128)(2,1)} %v_ref.7), custom_call_target="tpu_custom_call" | custom-call | flops 536870912 | bytes 4718592 | tf_op jit(solution)/shard_map/local_kernel/pallas_call | solution.py:30
  45.1 9.1 %all-to-all-done.1 = f32[64,8,128]{2,1,0:T(8,128)S(1)} async-done(((f32[64,8,128]{2,1,0:T(8,128)}), f32[64,8,128]{2,1,0:T(8,128)S(1)}, u32[]{:S(2)}, u32[]{:S(2)}) %all-to-all-start.1) | async-done | bytes 262176 | tf_op jit(solution)/shard_map/all_to_all | solution.py:183
  54.2 0.0 copy-start.1
  54.2 0.7 copy-done.1
  54.9 2.9 %stats_kernel.1 = (f32[512,512]{1,0:T(8,128)}, bf16[512,128]{1,0:T(8,128)(2,1)}, f32[8,8,128]{2,1,0:T(8,128)}) custom-call(bf16[512,512]{1,0:T(8,128)(2,1)} %q_ref.7, f32[512,512]{1,0:T(8,128)} %get-tuple-element.17.local_ref, f32[512,128]{1,0:T(8,128)} %bitcast.12, bf16[512,512]{1,0:T(8,128)(2,1)} %cot_ref.3, f32[1,512]{1,0:T(1,128)} %bitcast.14), custom_call_target="tpu_custom_call" | custom-call | flops 67108864 | bytes 3573760 | tf_op jit(solution)/shard_map/stats_kernel/pallas_call | solution.py:30
  57.8 9.8 %all_to_all.26.stats_ref = f32[8,8,128]{2,1,0:T(8,128)} all-to-all(f32[8,8,128]{2,1,0:T(8,128)} %get-tuple-element.19), channel_id=1, replica_groups=mesh['seq'=64,'fsdp'=8] {'fsdp'}, dimensions={0} | all-to-all | bytes 65536 | tf_op jit(solution)/shard_map/all_to_all | solution.py:225
  67.6 3.0 %grads_kernel.1 = (bf16[512,512]{1,0:T(8,128)(2,1)}, f32[576,128]{1,0:T(8,128)}) custom-call(f32[512,512]{1,0:T(8,128)} %get-tuple-element.18.att_ref, bf16[512,512]{1,0:T(8,128)(2,1)} %cot_ref.3, f32[1,512]{1,0:T(1,128)} %bitcast.15, f32[8,8,128]{2,1,0:T(8,128)} %all_to_all.26.stats_ref, bf16[512,512]{1,0:T(8,128)(2,1)} %q_ref.7), custom_call_target="tpu_custom_call" | custom-call | flops 67108864 | bytes 2951168 | tf_op jit(solution)/shard_map/grads_kernel/pallas_call | solution.py:30
  70.6 21.2 %all_to_all.27 = f32[64,9,1,128]{3,2,1,0:T(1,128)} all-to-all(f32[64,9,1,128]{3,2,1,0:T(1,128)} %bitcast.13), channel_id=1, replica_groups=mesh['seq'=64,'fsdp'=8] {'seq'}, dimensions={0} | all-to-all | bytes 589824 | tf_op jit(solution)/shard_map/all_to_all | solution.py:183
  91.8 1.8 %suffix_kernel.1 = f32[576,128]{1,0:T(8,128)} custom-call(f32[576,128]{1,0:T(8,128)} %bitcast.9), custom_call_target="tpu_custom_call" | custom-call | flops 65536 | bytes 589824 | tf_op jit(solution)/shard_map/suffix_kernel/pallas_call | solution.py:30
  93.5 5.1 %all-to-all-start.4 = ((f32[64,9,1,128]{3,2,1,0:T(1,128)}), f32[64,9,1,128]{3,2,1,0:T(1,128)S(1)}, u32[]{:S(2)}, u32[]{:S(2)}) async-start(f32[64,9,1,128]{3,2,1,0:T(1,128)} %bitcast.8), calls=%async_computation.4 | async-start | bytes 589824 | tf_op jit(solution)/shard_map/all_to_all | solution.py:183
  98.6 5.8 %backward_kernel.1 = (bf16[512,512]{1,0:T(8,128)(2,1)}, f32[512,512]{1,0:T(8,128)}, f32[512,512]{1,0:T(8,128)}, bf16[512,512]{1,0:T(8,128)(2,1)}) custom-call(bf16[512,512]{1,0:T(8,128)(2,1)} %q_ref.7, bf16[512,512]{1,0:T(8,128)(2,1)} %k_ref.7, bf16[512,512]{1,0:T(8,128)(2,1)} %v_ref.7, bf16[512,512]{1,0:T(8,128)(2,1)} %get-tuple-element.20.grads_ref, ...), custom_call_target="tpu_custom_call" | custom-call | flops 1140850688 | bytes 7471104 | tf_op jit(solution)/shard_map/backward_kernel/pallas_call | solution.py:30
  104.5 8.3 %all-to-all-done.4 = f32[64,9,1,128]{3,2,1,0:T(1,128)S(1)} async-done(((f32[64,9,1,128]{3,2,1,0:T(1,128)}), f32[64,9,1,128]{3,2,1,0:T(1,128)S(1)}, u32[]{:S(2)}, u32[]{:S(2)}) %all-to-all-start.4) | async-done | bytes 294944 | tf_op jit(solution)/shard_map/all_to_all | solution.py:183
  112.8 0.0 copy-start
  112.8 0.7 copy-done
  113.5 3.3 %final_kernel.1 = (bf16[512,512]{1,0:T(8,128)(2,1)}, bf16[512,512]{1,0:T(8,128)(2,1)}, f32[4,128]{1,0:T(4,128)}) custom-call(f32[512,512]{1,0:T(8,128)} %get-tuple-element.24.key_ref, f32[512,512]{1,0:T(8,128)} %get-tuple-element.25.value_ref, bf16[512,512]{1,0:T(8,128)(2,1)} %k_ref.7, bf16[512,512]{1,0:T(8,128)(2,1)} %v_ref.7, f32[576,128]{1,0:T(8,128)} %bitcast.10), custom_call_target="tpu_custom_call" | custom-call | flops 134217728 | bytes 4491264 | tf_op jit(solution)/shard_map/final_kernel/pallas_call | solution.py:30
Async XLA Ops:
  35.6 18.6 %all-to-all-start.1 = ((f32[64,8,128]{2,1,0:T(8,128)}), f32[64,8,128]{2,1,0:T(8,128)S(1)}, u32[]{:S(2)}, u32[]{:S(2)}) async-start(f32[64,8,128]{2,1,0:T(8,128)} %prefix_kernel.1), calls=%async_computation.1 | async-start | bytes 524288 | tf_op jit(solution)/shard_map/all_to_all | solution.py:183
  54.2 0.7 copy-start.1
  93.5 19.2 %all-to-all-start.4 = ((f32[64,9,1,128]{3,2,1,0:T(1,128)}), f32[64,9,1,128]{3,2,1,0:T(1,128)S(1)}, u32[]{:S(2)}, u32[]{:S(2)}) async-start(f32[64,9,1,128]{3,2,1,0:T(1,128)} %bitcast.8), calls=%async_computation.4 | async-start | bytes 589824 | tf_op jit(solution)/shard_map/all_to_all | solution.py:183
  112.8 0.7 copy-start

commit v2 on v1

--- a/solution.py
+++ b/solution.py
@@ -12,10 +12,24 @@
 EPS = 1e-05
 F32 = jnp.float32
 BF16 = jnp.bfloat16
+VMEM, HBM = pltpu.VMEM, pltpu.HBM
+VMEM_LIMIT = 16 * 2**20
 ROWS = 8
 GAIN_ROWS = ROWS + 1
 
 
+SEQ_FIRST = 46
+FSDP_FIRST = 6
+
+
+def place_of(j, count):
+    return (j - SEQ_FIRST) % count
+
+
+def groups(first, count):
+    return [[(first + i) % count for i in range(count)]]
+
+
 def dot(a, b, over_a, over_b):
     return lax.dot_general(a, b, (((over_a,), (over_b,)), ((), ())), preferred_element_type=F32)
 
@@ -24,24 +38,44 @@
     return pl.ds(h * HEAD_DIM, HEAD_DIM)
 
 
-def call(kernel, outs, flops, *args):
-    out_bytes = sum(math.prod(o.shape) * o.dtype.itemsize for o in outs)
+def call(kernel, outs, flops, *args, scratch=(), homes=None, spaces=None):
+    out_bytes = sum(math.prod(o.shape) * jnp.dtype(o.dtype).itemsize for o in outs)
     in_bytes = sum(math.prod(a.shape) * a.dtype.itemsize for a in args)
     return pl.pallas_call(
         kernel,
         out_shape=tuple(outs),
-        in_specs=[pl.BlockSpec(memory_space=pltpu.VMEM)] * len(args),
-        out_specs=tuple(pl.BlockSpec(memory_space=pltpu.VMEM) for _ in outs),
+        scratch_shapes=list(scratch),
+        in_specs=[pl.BlockSpec(memory_space=s) for s in spaces or [pltpu.VMEM] * len(args)],
+        out_specs=tuple(pl.BlockSpec(memory_space=VMEM) for _ in outs),
         cost_estimate=pl.CostEstimate(
             flops=flops, transcendentals=0, bytes_accessed=in_bytes + out_bytes
         ),
+        compiler_params=pltpu.CompilerParams(vmem_limit_bytes=VMEM_LIMIT),
         name=kernel.__name__,
-    )(*args)
-
-
-def state_kernel(k_ref, v_ref, out_ref):
-    for h in range(k_ref.shape[1] // HEAD_DIM):
-        out_ref[pl.ds(h * HEAD_DIM, HEAD_DIM), :] = dot(k_ref[:, cols(h)], v_ref[:, cols(h)], 0, 0)
+    )(*map(pltpu.with_memory_space_constraint, args, homes or [VMEM] * len(args)))
+
+
+def state_kernel(k_hbm, v_hbm, out_ref, k_ref, v_ref, sems):
+    rows, width = k_ref.shape
+    heads = width // HEAD_DIM
+    parts = sems.shape[1]
+    part = rows // parts
+    copies = []
+    for i in range(parts):
+        mine = pl.ds(i * part, part)
+        for n, (source, target) in enumerate(((k_hbm, k_ref), (v_hbm, v_ref))):
+            copy = pltpu.make_async_copy(source.at[mine], target.at[mine], sems.at[n, i])
+            copy.start()
+            copies.append(copy)
+    states = [jnp.zeros((HEAD_DIM, HEAD_DIM), F32)] * heads
+    for i in range(parts):
+        copies[2 * i].wait()
+        copies[2 * i + 1].wait()
+        mine = pl.ds(i * part, part)
+        for h in range(heads):
+            states[h] = states[h] + dot(k_ref[mine, cols(h)], v_ref[mine, cols(h)], 0, 0)
+    for h in range(heads):
+        out_ref[pl.ds(h * HEAD_DIM, HEAD_DIM), :] = states[h]
 
 
 def masked(scores, first_row, first_col):
@@ -50,7 +84,7 @@
     return jnp.where(row >= col, scores, 0.0)
 
 
-def local_kernel(q_ref, k_ref, v_ref, weights_ref, local_ref):
+def local_kernel(q_ref, k_ref, v_ref, local_ref):
     rows = q_ref.shape[0]
     block = min(256, rows)
     for h in range(q_ref.shape[1] // HEAD_DIM):
@@ -59,15 +93,16 @@
             ends = (i + 1) * block
             scores = dot(q_ref[mine, cols(h)], k_ref[:ends, cols(h)], 1, 1)
             weights = masked(scores, i * block, 0).astype(BF16)
-            weights_ref[h, mine, :ends] = weights
             local_ref[mine, cols(h)] = dot(weights, v_ref[:ends, cols(h)], 1, 0)
 
 
 def prefix_kernel(in_ref, out_ref):
+    count = in_ref.shape[0]
     acc = jnp.zeros(in_ref.shape[1:], F32)
-    for j in range(in_ref.shape[0]):
-        out_ref[j] = acc
-        acc = acc + in_ref[j]
+    for j in range(count):
+        at = place_of(j, count)
+        out_ref[at] = acc
+        acc = acc + in_ref[at]
 
 
 def suffix_kernel(in_ref, out_ref):
@@ -75,20 +110,20 @@
     acc = jnp.zeros((ROWS, HEAD_DIM), F32)
     gain = jnp.zeros((1, HEAD_DIM), F32)
     for j in reversed(range(count)):
-        out_ref[pl.ds(j * GAIN_ROWS, ROWS), :] = acc
-        acc = acc + in_ref[pl.ds(j * GAIN_ROWS, ROWS), :]
-        gain = gain + in_ref[pl.ds(j * GAIN_ROWS + ROWS, 1), :]
+        at = place_of(j, count) * GAIN_ROWS
+        out_ref[pl.ds(at, ROWS), :] = acc
+        acc = acc + in_ref[pl.ds(at, ROWS), :]
+        gain = gain + in_ref[pl.ds(at + ROWS, 1), :]
     for j in range(count):
         out_ref[pl.ds(j * GAIN_ROWS + ROWS, 1), :] = gain
 
 
-def stats_kernel(q_ref, local_ref, prefix_ref, cot_ref, gain_ref, att_ref, low_ref, out_ref):
+def stats_kernel(q_ref, local_ref, prefix_ref, cot_ref, gain_ref, att_ref, out_ref):
     rows, width = q_ref.shape
     squares = jnp.zeros((rows, HEAD_DIM), F32)
     crossed = jnp.zeros((rows, HEAD_DIM), F32)
     for h in range(width // HEAD_DIM):
         low = prefix_ref[pl.ds(h * HEAD_DIM, HEAD_DIM), :].astype(BF16)
-        low_ref[pl.ds(h * HEAD_DIM, HEAD_DIM), :] = low
         att = local_ref[:, cols(h)] + dot(q_ref[:, cols(h)], low, 1, 0)
         att_ref[:, cols(h)] = att
         squares = squares + att * att
@@ -137,35 +172,38 @@
 
 
 def backward_kernel(
-    q_ref, k_ref, v_ref, grads_ref, weights_ref, low_ref, query_ref, key_ref, value_ref, score_ref
+    q_ref, k_ref, v_ref, grads_ref, prefix_ref, query_ref, key_ref, value_ref, weights_ref, score_ref
 ):
     rows = q_ref.shape[0]
     block = min(256, rows)
     for h in range(q_ref.shape[1] // HEAD_DIM):
-        low = low_ref[pl.ds(h * HEAD_DIM, HEAD_DIM), :]
+        low = prefix_ref[pl.ds(h * HEAD_DIM, HEAD_DIM), :].astype(BF16)
         for i in range(rows // block):
             mine = pl.ds(i * block, block)
             ends = (i + 1) * block
-            scores = dot(grads_ref[mine, cols(h)], v_ref[:ends, cols(h)], 1, 1)
+            grads = grads_ref[mine, cols(h)]
+            keys = k_ref[:ends, cols(h)]
+            scores = dot(q_ref[mine, cols(h)], keys, 1, 1)
+            weights_ref[mine, :ends] = masked(scores, i * block, 0).astype(BF16)
+            scores = dot(grads, v_ref[:ends, cols(h)], 1, 1)
             score = masked(scores, i * block, 0).astype(BF16)
             score_ref[mine, :ends] = score
-            query = dot(score, k_ref[:ends, cols(h)], 1, 0)
-            query = query + dot(grads_ref[mine, cols(h)], low, 1, 1)
+            query = dot(score, keys, 1, 0) + dot(grads, low, 1, 1)
             query_ref[mine, cols(h)] = query.astype(BF16)
         for i in range(rows // block):
             mine = pl.ds(i * block, block)
             first = i * block
             key_ref[mine, cols(h)] = dot(score_ref[first:, mine], q_ref[first:, cols(h)], 0, 0)
             value_ref[mine, cols(h)] = dot(
-                weights_ref[h, first:, mine], grads_ref[first:, cols(h)], 0, 0
+                weights_ref[first:, mine], grads_ref[first:, cols(h)], 0, 0
             )
 
 
 def final_kernel(key_ref, value_ref, k_ref, v_ref, suffix_ref, key_out, value_out, gain_out):
-    heads = k_ref.shape[1] // HEAD_DIM
+    rows, width = k_ref.shape
     slices = HEAD_DIM // ROWS
-    length = suffix_ref.shape[0] // GAIN_ROWS * k_ref.shape[0]
-    for h in range(heads):
+    length = suffix_ref.shape[0] // GAIN_ROWS * rows
+    for h in range(width // HEAD_DIM):
         pieces = [
             suffix_ref[pl.ds((h * slices + s) * GAIN_ROWS, ROWS), :] for s in range(slices)
         ]
@@ -178,9 +216,16 @@
         gain_out[pl.ds(h, 1), :] = line * (1.0 / math.sqrt(length))
 
 
-def exchange(x, axis, shape):
+def exchange(x, axis, first, shape):
     count = lax.axis_size(axis)
-    moved = lax.all_to_all(x.reshape((count,) + shape), axis, 0, 0, tiled=True)
+    moved = lax.all_to_all(
+        x.reshape((count,) + shape),
+        axis,
+        0,
+        0,
+        axis_index_groups=groups(first, count),
+        tiled=True,
+    )
     return moved.reshape(x.shape)
 
 
@@ -189,31 +234,44 @@
     heads = width // HEAD_DIM
     blocks = lax.axis_size("seq")
     peers = lax.axis_size("fsdp")
-    sds = jax.ShapeDtypeStruct
+    sds, vmem = jax.ShapeDtypeStruct, pltpu.VMEM
     gain_row = gain.reshape(1, width)
     small = 2 * rows * width * HEAD_DIM
     big = 2 * rows * rows * width
 
-    (state,) = call(state_kernel, [sds((width, HEAD_DIM), F32)], small, key, value)
-    slices = exchange(state, "seq", (ROWS, HEAD_DIM))
-    weights, local = call(
+    (state,) = call(
+        state_kernel,
+        [vmem((width, HEAD_DIM), F32)],
+        small,
+        key,
+        value,
+        scratch=[
+            VMEM((rows, width), BF16),
+            VMEM((rows, width), BF16),
+            pltpu.SemaphoreType.DMA((2, 2)),
+        ],
+        homes=[HBM] * 2,
+        spaces=[HBM] * 2,
+    )
+    slices = exchange(state, "seq", SEQ_FIRST, (ROWS, HEAD_DIM))
+    (local,) = call(
         local_kernel,
-        [sds((heads, rows, rows), BF16), sds((rows, width), F32)],
+        [vmem((rows, width), F32)],
         2 * big,
         query,
         key,
         value,
+        homes=[HBM] * 3,
     )
     slices = slices.reshape(blocks, ROWS, HEAD_DIM)
-    (slices,) = call(prefix_kernel, [sds(slices.shape, F32)], width * HEAD_DIM, slices)
-    prefix = exchange(slices.reshape(width, HEAD_DIM), "seq", (ROWS, HEAD_DIM))
-
-    attended, prefix_low, stats = call(
+    (slices,) = call(prefix_kernel, [vmem(slices.shape, F32)], width * HEAD_DIM, slices)
+    prefix = exchange(slices.reshape(width, HEAD_DIM), "seq", SEQ_FIRST, (ROWS, HEAD_DIM))
+
+    attended, stats = call(
         stats_kernel,
         [
-            sds((rows, width), F32),
-            sds((width, HEAD_DIM), BF16),
-            sds((peers, 2 * rows // HEAD_DIM, HEAD_DIM), F32),
+            vmem((rows, width), F32),
+            vmem((peers, 2 * rows // HEAD_DIM, HEAD_DIM), F32),
         ],
         small,
         query,
@@ -222,10 +280,10 @@
         cotangent,
         gain_row,
     )
-    stats = lax.all_to_all(stats, "fsdp", 0, 0, tiled=True)
+    stats = exchange(stats, "fsdp", FSDP_FIRST, stats.shape[1:])
     grads, grad_state = call(
         grads_kernel,
-        [sds((rows, width), BF16), sds((blocks * GAIN_ROWS, HEAD_DIM), F32)],
+        [vmem((rows, width), BF16), sds((blocks * GAIN_ROWS, HEAD_DIM), F32)],
         small,
         attended,
         cotangent,
@@ -233,27 +291,27 @@
         stats,
         query,
     )
-    grad_slices = exchange(grad_state, "seq", (GAIN_ROWS, 1, HEAD_DIM))
-    query_grad, key_local, value_local, _ = call(
+    grad_slices = exchange(grad_state, "seq", SEQ_FIRST, (GAIN_ROWS, 1, HEAD_DIM))
+    query_grad, key_local, value_local = call(
         backward_kernel,
         [
             sds((rows, width), BF16),
-            sds((rows, width), F32),
-            sds((rows, width), F32),
-            sds((rows, rows), BF16),
+            vmem((rows, width), F32),
+            vmem((rows, width), F32),
         ],
         4 * big + small,
         query,
         key,
         value,
         grads,
-        weights,
-        prefix_low,
+        prefix,
+        scratch=[VMEM((rows, rows), BF16), VMEM((rows, rows), BF16)],
+        homes=[HBM] * 5,
     )
     (grad_slices,) = call(
-        suffix_kernel, [sds(grad_slices.shape, F32)], width * HEAD_DIM, grad_slices
-    )
-    suffix = exchange(grad_slices, "seq", (GAIN_ROWS, 1, HEAD_DIM))
+        suffix_kernel, [vmem(grad_slices.shape, F32)], width * HEAD_DIM, grad_slices
+    )
+    suffix = exchange(grad_slices, "seq", SEQ_FIRST, (GAIN_ROWS, 1, HEAD_DIM))
     key_grad, value_grad, gain_grad = call(
         final_kernel,
         [

time: 117 us -> 99.9 us (0.85)
  the two profiles are of different devices: /device:TPU:8 before, /device:TPU:56 now
where the time goes in v2:
time: 99.9 us; the launch traced here: 99.5 us
  blocking collectives  54.6 us (55%)
  starting transfers between devices  16.7 us (17%)
  Pallas kernels  13.7 us (14%)
  waiting for transfers between devices  13.6 us (14%)
    all_to_all x3, blocking collectives, exchange(): lax.all_to_all(x.reshape((count,) + shape), axis, 0, 0, axis_index_groups...  54.6 us
    all_to_all x2, starting transfers between devices, exchange(): lax.all_to_all(x.reshape((count,) + shape), axis, 0, 0, axis_index_groups...  16.7 us
    pallas_call x8, Pallas kernels, call(): pl.pallas_call(kernel, out_shape=tuple(outs), scratch_shapes=list(scratch...  13.7 us
    all_to_all x2, waiting for transfers between devices, exchange(): lax.all_to_all(x.reshape((count,) + shape), axis, 0, 0, axis_index_groups...  13.6 us
  transfers between devices with their start and end apart: 2, of which 2 were waited for; matrix products, arithmetic and copies ran while one was open for 0% of the time, Pallas kernels for 8%

profile of v2, /device:TPU:56, one launch (start us, length us, event | category | flops | bytes accessed | tf_op | source)
XLA Modules:
  0.0 99.5 jit_solution(2763200876520492572)
XLA Ops:
  0.6 1.6 %state_kernel.1 = f32[512,128]{1,0:T(8,128)S(1)} custom-call(bf16[512,512]{1,0:T(8,128)(2,1)} %k_ref.5, bf16[512,512]{1,0:T(8,128)(2,1)} %v_ref.5), custom_call_target="tpu_custom_call" | custom-call | flops 67108864 | bytes 1310720 | tf_op jit(solution)/shard_map/state_kernel/pallas_call | solution.py:44
  2.2 26.5 %all_to_all.25.in_ref = f32[64,8,128]{2,1,0:T(8,128)S(1)} all-to-all(f32[64,8,128]{2,1,0:T(8,128)S(1)} %bitcast.10), channel_id=1, replica_groups={{368,376,384,392,400,408,416,424,432,440,448,456,464,472,480,488,496,50..., dimensions={0} | all-to-all | bytes 524288 | tf_op jit(solution)/shard_map/all_to_all | solution.py:221
  28.7 0.8 prefix_kernel.1
  29.5 8.4 %all-to-all-start.1 = ((f32[64,8,128]{2,1,0:T(8,128)}), f32[64,8,128]{2,1,0:T(8,128)S(1)}, u32[]{:S(2)}, u32[]{:S(2)}) async-start(f32[64,8,128]{2,1,0:T(8,128)} %prefix_kernel.1), calls=%async_computation.1 | async-start | bytes 524288 | tf_op jit(solution)/shard_map/all_to_all | solution.py:221
  37.9 0.0 copy-start
  37.9 0.0 copy-start.3
  37.9 2.9 %local_kernel.1.local_ref = f32[512,512]{1,0:T(8,128)S(1)} custom-call(bf16[512,512]{1,0:T(8,128)(2,1)} %q_ref.7, bf16[512,512]{1,0:T(8,128)(2,1)} %k_ref.5, bf16[512,512]{1,0:T(8,128)(2,1)} %v_ref.5), custom_call_target="tpu_custom_call" | custom-call | flops 536870912 | bytes 2621440 | tf_op jit(solution)/shard_map/local_kernel/pallas_call | solution.py:44
  40.8 0.0 copy-start.5
  40.8 7.4 %all-to-all-done.1 = f32[64,8,128]{2,1,0:T(8,128)S(1)} async-done(((f32[64,8,128]{2,1,0:T(8,128)}), f32[64,8,128]{2,1,0:T(8,128)S(1)}, u32[]{:S(2)}, u32[]{:S(2)}) %all-to-all-start.1) | async-done | bytes 262176 | tf_op jit(solution)/shard_map/all_to_all | solution.py:221
  48.3 0.0 copy-done
  48.3 0.0 copy-done.3
  48.3 0.5 stats_kernel.1
  48.8 0.2 copy-done.4
  49.0 8.6 %all_to_all.26.stats_ref = f32[8,8,128]{2,1,0:T(8,128)S(1)} all-to-all(f32[8,8,128]{2,1,0:T(8,128)S(1)} %get-tuple-element.15), channel_id=1, replica_groups={{6,7,0,1,2,3,4,5},{14,15,8,9,10,11,12,13},{22,23,16,17,18,19,20,21},{30..., dimensions={0} | all-to-all | bytes 65536 | tf_op jit(solution)/shard_map/all_to_all | solution.py:221
  57.6 0.7 grads_kernel.1
  58.3 0.0 copy-start.6
  58.3 19.5 %all_to_all.27 = f32[64,9,1,128]{3,2,1,0:T(1,128)S(1)} all-to-all(f32[64,9,1,128]{3,2,1,0:T(1,128)S(1)} %bitcast.13), channel_id=1, replica_groups={{368,376,384,392,400,408,416,424,432,440,448,456,464,472,480,488,496,50..., dimensions={0} | all-to-all | bytes 589824 | tf_op jit(solution)/shard_map/all_to_all | solution.py:221
  77.8 0.8 suffix_kernel.1
  78.6 8.3 %all-to-all-start.4 = ((f32[64,9,1,128]{3,2,1,0:T(1,128)}), f32[64,9,1,128]{3,2,1,0:T(1,128)S(1)}, u32[]{:S(2)}, u32[]{:S(2)}) async-start(f32[64,9,1,128]{3,2,1,0:T(1,128)} %bitcast.5), calls=%async_computation.4 | async-start | bytes 589824 | tf_op jit(solution)/shard_map/all_to_all | solution.py:221
  86.9 0.0 copy-start.1
  86.9 0.0 copy-start.2
  86.9 5.0 %backward_kernel.1 = (bf16[512,512]{1,0:T(8,128)(2,1)}, f32[512,512]{1,0:T(8,128)S(1)}, f32[512,512]{1,0:T(8,128)S(1)}) custom-call(bf16[512,512]{1,0:T(8,128)(2,1)} %q_ref.7, bf16[512,512]{1,0:T(8,128)(2,1)} %k_ref.5, bf16[512,512]{1,0:T(8,128)(2,1)} %v_ref.5, bf16[512,512]{1,0:T(8,128)(2,1)} %copy-done.6, f32[512,128]{1,0:T(8,128)} %bitcast.12), custom_call_target="tpu_custom_call" | custom-call | flops 1140850688 | bytes 4980736 | tf_op jit(solution)/shard_map/backward_kernel/pallas_call | solution.py:44
  92.0 6.1 %all-to-all-done.4 = f32[64,9,1,128]{3,2,1,0:T(1,128)S(1)} async-done(((f32[64,9,1,128]{3,2,1,0:T(1,128)}), f32[64,9,1,128]{3,2,1,0:T(1,128)S(1)}, u32[]{:S(2)}, u32[]{:S(2)}) %all-to-all-start.4) | async-done | bytes 294944 | tf_op jit(solution)/shard_map/all_to_all | solution.py:221
  98.1 1.4 %final_kernel.1 = (bf16[512,512]{1,0:T(8,128)(2,1)}, bf16[512,512]{1,0:T(8,128)(2,1)}, f32[4,128]{1,0:T(4,128)}) custom-call(f32[512,512]{1,0:T(8,128)S(1)} %get-tuple-element.18.key_ref, f32[512,512]{1,0:T(8,128)S(1)} %get-tuple-element.19.value_ref, bf16[512,512]{1,0:T(8,128)(2,1)S(1)} %copy-done.1, bf16[512,512]{1,0:T(8,128)(2,1)S(1)} %copy-done.2, ...), custom_call_target="tpu_custom_call" | custom-call | flops 134217728 | bytes 4491264 | tf_op jit(solution)/shard_map/final_kernel/pallas_call | solution.py:44
  (5 shorter events, 0.0 us)
Async XLA Ops:
  29.5 18.8 %all-to-all-start.1 = ((f32[64,8,128]{2,1,0:T(8,128)}), f32[64,8,128]{2,1,0:T(8,128)S(1)}, u32[]{:S(2)}, u32[]{:S(2)}) async-start(f32[64,8,128]{2,1,0:T(8,128)} %prefix_kernel.1), calls=%async_computation.1 | async-start | bytes 524288 | tf_op jit(solution)/shard_map/all_to_all | solution.py:221
  37.9 10.4 %copy-start = (bf16[512,512]{1,0:T(8,128)(2,1)S(1)}, bf16[512,512]{1,0:T(8,128)(2,1)}, u32[]{:S(2)}) copy-start(bf16[512,512]{1,0:T(8,128)(2,1)} %q_ref.7) | copy-start | bytes 1572868
  37.9 10.4 %copy-start.3 = (bf16[512,512]{1,0:T(8,128)(2,1)S(1)}, bf16[512,512]{1,0:T(8,128)(2,1)}, u32[]{:S(2)}) copy-start(bf16[512,512]{1,0:T(8,128)(2,1)} %cot_ref.3) | copy-start | bytes 1572868
  40.8 7.5 %copy-start.5 = (f32[512]{0:T(512)S(1)}, f32[512]{0:T(512)}, u32[]{:S(2)}) copy-start(f32[512]{0:T(512)} %param.9) | copy-start | bytes 6148
  48.3 0.7 copy-start.4
  58.3 20.3 %copy-start.6 = (bf16[512,512]{1,0:T(8,128)(2,1)}, bf16[512,512]{1,0:T(8,128)(2,1)S(1)}, u32[]{:S(2)}) copy-start(bf16[512,512]{1,0:T(8,128)(2,1)S(1)} %get-tuple-element.16.grads_ref) | copy-start | bytes 1572868
  78.6 19.5 %all-to-all-start.4 = ((f32[64,9,1,128]{3,2,1,0:T(1,128)}), f32[64,9,1,128]{3,2,1,0:T(1,128)S(1)}, u32[]{:S(2)}, u32[]{:S(2)}) async-start(f32[64,9,1,128]{3,2,1,0:T(1,128)} %bitcast.5), calls=%async_computation.4 | async-start | bytes 589824 | tf_op jit(solution)/shard_map/all_to_all | solution.py:221
  86.9 11.2 %copy-start.1 = (bf16[512,512]{1,0:T(8,128)(2,1)S(1)}, bf16[512,512]{1,0:T(8,128)(2,1)}, u32[]{:S(2)}) copy-start(bf16[512,512]{1,0:T(8,128)(2,1)} %k_ref.5) | copy-start | bytes 1572868
  86.9 11.2 %copy-start.2 = (bf16[512,512]{1,0:T(8,128)(2,1)S(1)}, bf16[512,512]{1,0:T(8,128)(2,1)}, u32[]{:S(2)}) copy-start(bf16[512,512]{1,0:T(8,128)(2,1)} %v_ref.5) | copy-start | bytes 1572868

commit v3 on v2

--- a/solution.py
+++ b/solution.py
@@ -16,10 +16,8 @@
 VMEM_LIMIT = 16 * 2**20
 ROWS = 8
 GAIN_ROWS = ROWS + 1
-
-
-SEQ_FIRST = 46
-FSDP_FIRST = 6
+SEQ_FIRST = 45
+FSDP_FIRST = 4
 
 
 def place_of(j, count):

time: 99.9 us -> 98.8 us (0.989)
  waiting for transfers between devices: 13.6 us -> 11.3 us
  starting transfers between devices: 16.7 us -> 18.7 us
  blocking collectives: 54.6 us -> 53.1 us
    all_to_all x2, waiting for transfers between devices: 13.6 us -> 11.3 us  [exchange(): lax.all_to_all(x.reshape((count,) + shape), axis, 0, 0, axis_index_groups...]
    all_to_all x2, starting transfers between devices: 16.7 us -> 18.7 us  [exchange(): lax.all_to_all(x.reshape((count,) + shape), axis, 0, 0, axis_index_groups...]
    all_to_all x3, blocking collectives: 54.6 us -> 53.1 us  [exchange(): lax.all_to_all(x.reshape((count,) + shape), axis, 0, 0, axis_index_groups...]
where the time goes in v3:
time: 98.8 us; the launch traced here: 97.8 us
  blocking collectives  53.1 us (54%)
  starting transfers between devices  18.7 us (19%)
  Pallas kernels  13.7 us (14%)
  waiting for transfers between devices  11.3 us (11%)
    all_to_all x3, blocking collectives, exchange(): lax.all_to_all(x.reshape((count,) + shape), axis, 0, 0, axis_index_groups...  53.1 us
    all_to_all x2, starting transfers between devices, exchange(): lax.all_to_all(x.reshape((count,) + shape), axis, 0, 0, axis_index_groups...  18.7 us
    pallas_call x8, Pallas kernels, call(): pl.pallas_call(kernel, out_shape=tuple(outs), scratch_shapes=list(scratch...  13.7 us
    all_to_all x2, waiting for transfers between devices, exchange(): lax.all_to_all(x.reshape((count,) + shape), axis, 0, 0, axis_index_groups...  11.3 us
  transfers between devices with their start and end apart: 2, of which 2 were waited for; matrix products, arithmetic and copies ran while one was open for 0% of the time, Pallas kernels for 8%

profile of v3, /device:TPU:56, one launch (start us, length us, event | category | flops | bytes accessed | tf_op | source)
XLA Modules:
  0.0 97.8 jit_solution(7510349770525618110)
XLA Ops:
  0.6 1.6 %state_kernel.1 = f32[512,128]{1,0:T(8,128)S(1)} custom-call(bf16[512,512]{1,0:T(8,128)(2,1)} %k_ref.5, bf16[512,512]{1,0:T(8,128)(2,1)} %v_ref.5), custom_call_target="tpu_custom_call" | custom-call | flops 67108864 | bytes 1310720 | tf_op jit(solution)/shard_map/state_kernel/pallas_call | solution.py:42
  2.2 25.7 %all_to_all.25.in_ref = f32[64,8,128]{2,1,0:T(8,128)S(1)} all-to-all(f32[64,8,128]{2,1,0:T(8,128)S(1)} %bitcast.10), channel_id=1, replica_groups={{360,368,376,384,392,400,408,416,424,432,440,448,456,464,472,480,488,49..., dimensions={0} | all-to-all | bytes 524288 | tf_op jit(solution)/shard_map/all_to_all | solution.py:219
  27.9 0.8 prefix_kernel.1
  28.7 9.4 %all-to-all-start.1 = ((f32[64,8,128]{2,1,0:T(8,128)}), f32[64,8,128]{2,1,0:T(8,128)S(1)}, u32[]{:S(2)}, u32[]{:S(2)}) async-start(f32[64,8,128]{2,1,0:T(8,128)} %prefix_kernel.1), calls=%async_computation.1 | async-start | bytes 524288 | tf_op jit(solution)/shard_map/all_to_all | solution.py:219
  38.0 0.0 copy-start
  38.0 0.0 copy-start.3
  38.0 2.9 %local_kernel.1.local_ref = f32[512,512]{1,0:T(8,128)S(1)} custom-call(bf16[512,512]{1,0:T(8,128)(2,1)} %q_ref.7, bf16[512,512]{1,0:T(8,128)(2,1)} %k_ref.5, bf16[512,512]{1,0:T(8,128)(2,1)} %v_ref.5), custom_call_target="tpu_custom_call" | custom-call | flops 536870912 | bytes 2621440 | tf_op jit(solution)/shard_map/local_kernel/pallas_call | solution.py:42
  40.9 0.0 copy-start.5
  40.9 6.4 %all-to-all-done.1 = f32[64,8,128]{2,1,0:T(8,128)S(1)} async-done(((f32[64,8,128]{2,1,0:T(8,128)}), f32[64,8,128]{2,1,0:T(8,128)S(1)}, u32[]{:S(2)}, u32[]{:S(2)}) %all-to-all-start.1) | async-done | bytes 262176 | tf_op jit(solution)/shard_map/all_to_all | solution.py:219
  47.4 0.0 copy-done
  47.4 0.5 stats_kernel.1
  47.9 0.2 copy-done.4
  48.1 7.8 %all_to_all.26.stats_ref = f32[8,8,128]{2,1,0:T(8,128)S(1)} all-to-all(f32[8,8,128]{2,1,0:T(8,128)S(1)} %get-tuple-element.15), channel_id=1, replica_groups={{4,5,6,7,0,1,2,3},{12,13,14,15,8,9,10,11},{20,21,22,23,16,17,18,19},{28..., dimensions={0} | all-to-all | bytes 65536 | tf_op jit(solution)/shard_map/all_to_all | solution.py:219
  55.8 0.7 grads_kernel.1
  56.6 0.0 copy-start.6
  56.6 19.7 %all_to_all.27 = f32[64,9,1,128]{3,2,1,0:T(1,128)S(1)} all-to-all(f32[64,9,1,128]{3,2,1,0:T(1,128)S(1)} %bitcast.13), channel_id=1, replica_groups={{360,368,376,384,392,400,408,416,424,432,440,448,456,464,472,480,488,49..., dimensions={0} | all-to-all | bytes 589824 | tf_op jit(solution)/shard_map/all_to_all | solution.py:219
  76.2 0.8 suffix_kernel.1
  77.0 9.4 %all-to-all-start.4 = ((f32[64,9,1,128]{3,2,1,0:T(1,128)}), f32[64,9,1,128]{3,2,1,0:T(1,128)S(1)}, u32[]{:S(2)}, u32[]{:S(2)}) async-start(f32[64,9,1,128]{3,2,1,0:T(1,128)} %bitcast.5), calls=%async_computation.4 | async-start | bytes 589824 | tf_op jit(solution)/shard_map/all_to_all | solution.py:219
  86.4 0.0 copy-start.1
  86.4 0.0 copy-start.2
  86.4 5.0 %backward_kernel.1 = (bf16[512,512]{1,0:T(8,128)(2,1)}, f32[512,512]{1,0:T(8,128)S(1)}, f32[512,512]{1,0:T(8,128)S(1)}) custom-call(bf16[512,512]{1,0:T(8,128)(2,1)} %q_ref.7, bf16[512,512]{1,0:T(8,128)(2,1)} %k_ref.5, bf16[512,512]{1,0:T(8,128)(2,1)} %v_ref.5, bf16[512,512]{1,0:T(8,128)(2,1)} %copy-done.6, f32[512,128]{1,0:T(8,128)} %bitcast.12), custom_call_target="tpu_custom_call" | custom-call | flops 1140850688 | bytes 4980736 | tf_op jit(solution)/shard_map/backward_kernel/pallas_call | solution.py:42
  91.5 4.9 %all-to-all-done.4 = f32[64,9,1,128]{3,2,1,0:T(1,128)S(1)} async-done(((f32[64,9,1,128]{3,2,1,0:T(1,128)}), f32[64,9,1,128]{3,2,1,0:T(1,128)S(1)}, u32[]{:S(2)}, u32[]{:S(2)}) %all-to-all-start.4) | async-done | bytes 294944 | tf_op jit(solution)/shard_map/all_to_all | solution.py:219
  96.3 0.0 copy-done.2
  96.3 1.4 %final_kernel.1 = (bf16[512,512]{1,0:T(8,128)(2,1)}, bf16[512,512]{1,0:T(8,128)(2,1)}, f32[4,128]{1,0:T(4,128)}) custom-call(f32[512,512]{1,0:T(8,128)S(1)} %get-tuple-element.18.key_ref, f32[512,512]{1,0:T(8,128)S(1)} %get-tuple-element.19.value_ref, bf16[512,512]{1,0:T(8,128)(2,1)S(1)} %copy-done.1, bf16[512,512]{1,0:T(8,128)(2,1)S(1)} %copy-done.2, ...), custom_call_target="tpu_custom_call" | custom-call | flops 134217728 | bytes 4491264 | tf_op jit(solution)/shard_map/final_kernel/pallas_call | solution.py:42
  (5 shorter events, 0.0 us)
Async XLA Ops:
  28.7 18.7 %all-to-all-start.1 = ((f32[64,8,128]{2,1,0:T(8,128)}), f32[64,8,128]{2,1,0:T(8,128)S(1)}, u32[]{:S(2)}, u32[]{:S(2)}) async-start(f32[64,8,128]{2,1,0:T(8,128)} %prefix_kernel.1), calls=%async_computation.1 | async-start | bytes 524288 | tf_op jit(solution)/shard_map/all_to_all | solution.py:219
  38.0 9.3 %copy-start = (bf16[512,512]{1,0:T(8,128)(2,1)S(1)}, bf16[512,512]{1,0:T(8,128)(2,1)}, u32[]{:S(2)}) copy-start(bf16[512,512]{1,0:T(8,128)(2,1)} %q_ref.7) | copy-start | bytes 1572868
  38.0 9.3 %copy-start.3 = (bf16[512,512]{1,0:T(8,128)(2,1)S(1)}, bf16[512,512]{1,0:T(8,128)(2,1)}, u32[]{:S(2)}) copy-start(bf16[512,512]{1,0:T(8,128)(2,1)} %cot_ref.3) | copy-start | bytes 1572868
  40.9 6.4 %copy-start.5 = (f32[512]{0:T(512)S(1)}, f32[512]{0:T(512)}, u32[]{:S(2)}) copy-start(f32[512]{0:T(512)} %param.9) | copy-start | bytes 6148
  47.4 0.7 copy-start.4
  56.6 20.5 %copy-start.6 = (bf16[512,512]{1,0:T(8,128)(2,1)}, bf16[512,512]{1,0:T(8,128)(2,1)S(1)}, u32[]{:S(2)}) copy-start(bf16[512,512]{1,0:T(8,128)(2,1)S(1)} %get-tuple-element.16.grads_ref) | copy-start | bytes 1572868
  77.0 19.3 %all-to-all-start.4 = ((f32[64,9,1,128]{3,2,1,0:T(1,128)}), f32[64,9,1,128]{3,2,1,0:T(1,128)S(1)}, u32[]{:S(2)}, u32[]{:S(2)}) async-start(f32[64,9,1,128]{3,2,1,0:T(1,128)} %bitcast.5), calls=%async_computation.4 | async-start | bytes 589824 | tf_op jit(solution)/shard_map/all_to_all | solution.py:219
  86.4 9.9 %copy-start.1 = (bf16[512,512]{1,0:T(8,128)(2,1)S(1)}, bf16[512,512]{1,0:T(8,128)(2,1)}, u32[]{:S(2)}) copy-start(bf16[512,512]{1,0:T(8,128)(2,1)} %k_ref.5) | copy-start | bytes 1572868
  86.4 9.9 %copy-start.2 = (bf16[512,512]{1,0:T(8,128)(2,1)S(1)}, bf16[512,512]{1,0:T(8,128)(2,1)}, u32[]{:S(2)}) copy-start(bf16[512,512]{1,0:T(8,128)(2,1)} %v_ref.5) | copy-start | bytes 1572868

commit v4 on v3

--- a/solution.py
+++ b/solution.py
@@ -16,8 +16,8 @@
 VMEM_LIMIT = 16 * 2**20
 ROWS = 8
 GAIN_ROWS = ROWS + 1
-SEQ_FIRST = 45
-FSDP_FIRST = 4
+SEQ_FIRST = 37
+FSDP_FIRST = 5
 
 
 def place_of(j, count):

time: 98.8 us -> 98.1 us (level)
  no operation moved by 1% of the time
where the time goes in v4:
time: 98.1 us; the launch traced here: 97.4 us
  blocking collectives  52.9 us (54%)
  starting transfers between devices  19.5 us (20%)
  Pallas kernels  13.7 us (14%)
  waiting for transfers between devices  10.4 us (11%)
    all_to_all x3, blocking collectives, exchange(): lax.all_to_all(x.reshape((count,) + shape), axis, 0, 0, axis_index_groups...  52.9 us
    all_to_all x2, starting transfers between devices, exchange(): lax.all_to_all(x.reshape((count,) + shape), axis, 0, 0, axis_index_groups...  19.5 us
    pallas_call x8, Pallas kernels, call(): pl.pallas_call(kernel, out_shape=tuple(outs), scratch_shapes=list(scratch...  13.7 us
    all_to_all x2, waiting for transfers between devices, exchange(): lax.all_to_all(x.reshape((count,) + shape), axis, 0, 0, axis_index_groups...  10.4 us
  transfers between devices with their start and end apart: 2, of which 2 were waited for; matrix products, arithmetic and copies ran while one was open for 0% of the time, Pallas kernels for 8%

profile of v4, /device:TPU:56, one launch (start us, length us, event | category | flops | bytes accessed | tf_op | source)
XLA Modules:
  0.0 97.4 jit_solution(5502014682969545395)
XLA Ops:
  0.6 1.6 %state_kernel.1 = f32[512,128]{1,0:T(8,128)S(1)} custom-call(bf16[512,512]{1,0:T(8,128)(2,1)} %k_ref.5, bf16[512,512]{1,0:T(8,128)(2,1)} %v_ref.5), custom_call_target="tpu_custom_call" | custom-call | flops 67108864 | bytes 1310720 | tf_op jit(solution)/shard_map/state_kernel/pallas_call | solution.py:42
  2.2 25.7 %all_to_all.25.in_ref = f32[64,8,128]{2,1,0:T(8,128)S(1)} all-to-all(f32[64,8,128]{2,1,0:T(8,128)S(1)} %bitcast.10), channel_id=1, replica_groups={{296,304,312,320,328,336,344,352,360,368,376,384,392,400,408,416,424,43..., dimensions={0} | all-to-all | bytes 524288 | tf_op jit(solution)/shard_map/all_to_all | solution.py:219
  27.9 0.8 prefix_kernel.1
  28.7 9.7 %all-to-all-start.1 = ((f32[64,8,128]{2,1,0:T(8,128)}), f32[64,8,128]{2,1,0:T(8,128)S(1)}, u32[]{:S(2)}, u32[]{:S(2)}) async-start(f32[64,8,128]{2,1,0:T(8,128)} %prefix_kernel.1), calls=%async_computation.1 | async-start | bytes 524288 | tf_op jit(solution)/shard_map/all_to_all | solution.py:219
  38.4 0.0 copy-start
  38.4 0.0 copy-start.3
  38.4 2.9 %local_kernel.1.local_ref = f32[512,512]{1,0:T(8,128)S(1)} custom-call(bf16[512,512]{1,0:T(8,128)(2,1)} %q_ref.7, bf16[512,512]{1,0:T(8,128)(2,1)} %k_ref.5, bf16[512,512]{1,0:T(8,128)(2,1)} %v_ref.5), custom_call_target="tpu_custom_call" | custom-call | flops 536870912 | bytes 2621440 | tf_op jit(solution)/shard_map/local_kernel/pallas_call | solution.py:42
  41.3 0.0 copy-start.5
  41.3 6.0 %all-to-all-done.1 = f32[64,8,128]{2,1,0:T(8,128)S(1)} async-done(((f32[64,8,128]{2,1,0:T(8,128)}), f32[64,8,128]{2,1,0:T(8,128)S(1)}, u32[]{:S(2)}, u32[]{:S(2)}) %all-to-all-start.1) | async-done | bytes 262176 | tf_op jit(solution)/shard_map/all_to_all | solution.py:219
  47.3 0.0 copy-done
  47.3 0.0 copy-done.3
  47.3 0.5 stats_kernel.1
  47.8 0.2 copy-done.4
  48.0 7.4 %all_to_all.26.stats_ref = f32[8,8,128]{2,1,0:T(8,128)S(1)} all-to-all(f32[8,8,128]{2,1,0:T(8,128)S(1)} %get-tuple-element.15), channel_id=1, replica_groups={{5,6,7,0,1,2,3,4},{13,14,15,8,9,10,11,12},{21,22,23,16,17,18,19,20},{29..., dimensions={0} | all-to-all | bytes 65536 | tf_op jit(solution)/shard_map/all_to_all | solution.py:219
  55.4 0.7 grads_kernel.1
  56.1 0.0 copy-start.6
  56.1 19.7 %all_to_all.27 = f32[64,9,1,128]{3,2,1,0:T(1,128)S(1)} all-to-all(f32[64,9,1,128]{3,2,1,0:T(1,128)S(1)} %bitcast.13), channel_id=1, replica_groups={{296,304,312,320,328,336,344,352,360,368,376,384,392,400,408,416,424,43..., dimensions={0} | all-to-all | bytes 589824 | tf_op jit(solution)/shard_map/all_to_all | solution.py:219
  75.9 0.8 suffix_kernel.1
  76.7 9.8 %all-to-all-start.4 = ((f32[64,9,1,128]{3,2,1,0:T(1,128)}), f32[64,9,1,128]{3,2,1,0:T(1,128)S(1)}, u32[]{:S(2)}, u32[]{:S(2)}) async-start(f32[64,9,1,128]{3,2,1,0:T(1,128)} %bitcast.5), calls=%async_computation.4 | async-start | bytes 589824 | tf_op jit(solution)/shard_map/all_to_all | solution.py:219
  86.5 0.0 copy-start.1
  86.5 0.0 copy-start.2
  86.5 5.1 %backward_kernel.1 = (bf16[512,512]{1,0:T(8,128)(2,1)}, f32[512,512]{1,0:T(8,128)S(1)}, f32[512,512]{1,0:T(8,128)S(1)}) custom-call(bf16[512,512]{1,0:T(8,128)(2,1)} %q_ref.7, bf16[512,512]{1,0:T(8,128)(2,1)} %k_ref.5, bf16[512,512]{1,0:T(8,128)(2,1)} %v_ref.5, bf16[512,512]{1,0:T(8,128)(2,1)} %copy-done.6, f32[512,128]{1,0:T(8,128)} %bitcast.12), custom_call_target="tpu_custom_call" | custom-call | flops 1140850688 | bytes 4980736 | tf_op jit(solution)/shard_map/backward_kernel/pallas_call | solution.py:42
  91.5 4.5 %all-to-all-done.4 = f32[64,9,1,128]{3,2,1,0:T(1,128)S(1)} async-done(((f32[64,9,1,128]{3,2,1,0:T(1,128)}), f32[64,9,1,128]{3,2,1,0:T(1,128)S(1)}, u32[]{:S(2)}, u32[]{:S(2)}) %all-to-all-start.4) | async-done | bytes 294944 | tf_op jit(solution)/shard_map/all_to_all | solution.py:219
  96.0 1.4 %final_kernel.1 = (bf16[512,512]{1,0:T(8,128)(2,1)}, bf16[512,512]{1,0:T(8,128)(2,1)}, f32[4,128]{1,0:T(4,128)}) custom-call(f32[512,512]{1,0:T(8,128)S(1)} %get-tuple-element.18.key_ref, f32[512,512]{1,0:T(8,128)S(1)} %get-tuple-element.19.value_ref, bf16[512,512]{1,0:T(8,128)(2,1)S(1)} %copy-done.1, bf16[512,512]{1,0:T(8,128)(2,1)S(1)} %copy-done.2, ...), custom_call_target="tpu_custom_call" | custom-call | flops 134217728 | bytes 4491264 | tf_op jit(solution)/shard_map/final_kernel/pallas_call | solution.py:42
  (5 shorter events, 0.0 us)
Async XLA Ops:
  28.7 18.6 %all-to-all-start.1 = ((f32[64,8,128]{2,1,0:T(8,128)}), f32[64,8,128]{2,1,0:T(8,128)S(1)}, u32[]{:S(2)}, u32[]{:S(2)}) async-start(f32[64,8,128]{2,1,0:T(8,128)} %prefix_kernel.1), calls=%async_computation.1 | async-start | bytes 524288 | tf_op jit(solution)/shard_map/all_to_all | solution.py:219
  38.4 8.9 %copy-start = (bf16[512,512]{1,0:T(8,128)(2,1)S(1)}, bf16[512,512]{1,0:T(8,128)(2,1)}, u32[]{:S(2)}) copy-start(bf16[512,512]{1,0:T(8,128)(2,1)} %q_ref.7) | copy-start | bytes 1572868
  38.4 8.9 %copy-start.3 = (bf16[512,512]{1,0:T(8,128)(2,1)S(1)}, bf16[512,512]{1,0:T(8,128)(2,1)}, u32[]{:S(2)}) copy-start(bf16[512,512]{1,0:T(8,128)(2,1)} %cot_ref.3) | copy-start | bytes 1572868
  41.3 6.0 %copy-start.5 = (f32[512]{0:T(512)S(1)}, f32[512]{0:T(512)}, u32[]{:S(2)}) copy-start(f32[512]{0:T(512)} %param.9) | copy-start | bytes 6148
  47.3 0.7 copy-start.4
  56.1 20.6 %copy-start.6 = (bf16[512,512]{1,0:T(8,128)(2,1)}, bf16[512,512]{1,0:T(8,128)(2,1)S(1)}, u32[]{:S(2)}) copy-start(bf16[512,512]{1,0:T(8,128)(2,1)S(1)} %get-tuple-element.16.grads_ref) | copy-start | bytes 1572868
  76.7 19.3 %all-to-all-start.4 = ((f32[64,9,1,128]{3,2,1,0:T(1,128)}), f32[64,9,1,128]{3,2,1,0:T(1,128)S(1)}, u32[]{:S(2)}, u32[]{:S(2)}) async-start(f32[64,9,1,128]{3,2,1,0:T(1,128)} %bitcast.5), calls=%async_computation.4 | async-start | bytes 589824 | tf_op jit(solution)/shard_map/all_to_all | solution.py:219
  86.5 9.5 %copy-start.1 = (bf16[512,512]{1,0:T(8,128)(2,1)S(1)}, bf16[512,512]{1,0:T(8,128)(2,1)}, u32[]{:S(2)}) copy-start(bf16[512,512]{1,0:T(8,128)(2,1)} %k_ref.5) | copy-start | bytes 1572868
  86.5 9.5 %copy-start.2 = (bf16[512,512]{1,0:T(8,128)(2,1)S(1)}, bf16[512,512]{1,0:T(8,128)(2,1)}, u32[]{:S(2)}) copy-start(bf16[512,512]{1,0:T(8,128)(2,1)} %v_ref.5) | copy-start | bytes 1572868

commit v5 on v4

--- a/solution.py
+++ b/solution.py
@@ -246,7 +246,7 @@
         scratch=[
             VMEM((rows, width), BF16),
             VMEM((rows, width), BF16),
-            pltpu.SemaphoreType.DMA((2, 2)),
+            pltpu.SemaphoreType.DMA((2, 4)),
         ],
         homes=[HBM] * 2,
         spaces=[HBM] * 2,

time: 98.1 us -> 98.2 us (level)
  no operation moved by 1% of the time
where the time goes in v5:
time: 98.2 us; the launch traced here: 97.5 us
  blocking collectives  52.9 us (54%)
  starting transfers between devices  19.5 us (20%)
  Pallas kernels  13.8 us (14%)
  waiting for transfers between devices  10.4 us (11%)
    all_to_all x3, blocking collectives, exchange(): lax.all_to_all(x.reshape((count,) + shape), axis, 0, 0, axis_index_groups...  52.9 us
    all_to_all x2, starting transfers between devices, exchange(): lax.all_to_all(x.reshape((count,) + shape), axis, 0, 0, axis_index_groups...  19.5 us
    pallas_call x8, Pallas kernels, call(): pl.pallas_call(kernel, out_shape=tuple(outs), scratch_shapes=list(scratch...  13.8 us
    all_to_all x2, waiting for transfers between devices, exchange(): lax.all_to_all(x.reshape((count,) + shape), axis, 0, 0, axis_index_groups...  10.4 us
  transfers between devices with their start and end apart: 2, of which 2 were waited for; matrix products, arithmetic and copies ran while one was open for 0% of the time, Pallas kernels for 8%

profile of v5, /device:TPU:56, one launch (start us, length us, event | category | flops | bytes accessed | tf_op | source)
XLA Modules:
  0.0 97.5 jit_solution(9634885841435077977)
XLA Ops:
  0.6 1.6 %state_kernel.1 = f32[512,128]{1,0:T(8,128)S(1)} custom-call(bf16[512,512]{1,0:T(8,128)(2,1)} %k_ref.5, bf16[512,512]{1,0:T(8,128)(2,1)} %v_ref.5), custom_call_target="tpu_custom_call" | custom-call | flops 67108864 | bytes 1310720 | tf_op jit(solution)/shard_map/state_kernel/pallas_call | solution.py:42
  2.3 25.7 %all_to_all.25.in_ref = f32[64,8,128]{2,1,0:T(8,128)S(1)} all-to-all(f32[64,8,128]{2,1,0:T(8,128)S(1)} %bitcast.10), channel_id=1, replica_groups={{296,304,312,320,328,336,344,352,360,368,376,384,392,400,408,416,424,43..., dimensions={0} | all-to-all | bytes 524288 | tf_op jit(solution)/shard_map/all_to_all | solution.py:219
  28.0 0.8 prefix_kernel.1
  28.7 9.7 %all-to-all-start.1 = ((f32[64,8,128]{2,1,0:T(8,128)}), f32[64,8,128]{2,1,0:T(8,128)S(1)}, u32[]{:S(2)}, u32[]{:S(2)}) async-start(f32[64,8,128]{2,1,0:T(8,128)} %prefix_kernel.1), calls=%async_computation.1 | async-start | bytes 524288 | tf_op jit(solution)/shard_map/all_to_all | solution.py:219
  38.5 0.0 copy-start
  38.5 0.0 copy-start.3
  38.5 2.9 %local_kernel.1.local_ref = f32[512,512]{1,0:T(8,128)S(1)} custom-call(bf16[512,512]{1,0:T(8,128)(2,1)} %q_ref.7, bf16[512,512]{1,0:T(8,128)(2,1)} %k_ref.5, bf16[512,512]{1,0:T(8,128)(2,1)} %v_ref.5), custom_call_target="tpu_custom_call" | custom-call | flops 536870912 | bytes 2621440 | tf_op jit(solution)/shard_map/local_kernel/pallas_call | solution.py:42
  41.4 0.0 copy-start.5
  41.4 6.0 %all-to-all-done.1 = f32[64,8,128]{2,1,0:T(8,128)S(1)} async-done(((f32[64,8,128]{2,1,0:T(8,128)}), f32[64,8,128]{2,1,0:T(8,128)S(1)}, u32[]{:S(2)}, u32[]{:S(2)}) %all-to-all-start.1) | async-done | bytes 262176 | tf_op jit(solution)/shard_map/all_to_all | solution.py:219
  47.3 0.0 copy-done
  47.4 0.5 stats_kernel.1
  47.9 0.2 copy-done.4
  48.1 7.4 %all_to_all.26.stats_ref = f32[8,8,128]{2,1,0:T(8,128)S(1)} all-to-all(f32[8,8,128]{2,1,0:T(8,128)S(1)} %get-tuple-element.15), channel_id=1, replica_groups={{5,6,7,0,1,2,3,4},{13,14,15,8,9,10,11,12},{21,22,23,16,17,18,19,20},{29..., dimensions={0} | all-to-all | bytes 65536 | tf_op jit(solution)/shard_map/all_to_all | solution.py:219
  55.5 0.7 grads_kernel.1
  56.2 0.0 copy-start.6
  56.2 19.8 %all_to_all.27 = f32[64,9,1,128]{3,2,1,0:T(1,128)S(1)} all-to-all(f32[64,9,1,128]{3,2,1,0:T(1,128)S(1)} %bitcast.13), channel_id=1, replica_groups={{296,304,312,320,328,336,344,352,360,368,376,384,392,400,408,416,424,43..., dimensions={0} | all-to-all | bytes 589824 | tf_op jit(solution)/shard_map/all_to_all | solution.py:219
  75.9 0.8 suffix_kernel.1
  76.8 9.8 %all-to-all-start.4 = ((f32[64,9,1,128]{3,2,1,0:T(1,128)}), f32[64,9,1,128]{3,2,1,0:T(1,128)S(1)}, u32[]{:S(2)}, u32[]{:S(2)}) async-start(f32[64,9,1,128]{3,2,1,0:T(1,128)} %bitcast.5), calls=%async_computation.4 | async-start | bytes 589824 | tf_op jit(solution)/shard_map/all_to_all | solution.py:219
  86.5 0.0 copy-start.1
  86.5 0.0 copy-start.2
  86.5 5.1 %backward_kernel.1 = (bf16[512,512]{1,0:T(8,128)(2,1)}, f32[512,512]{1,0:T(8,128)S(1)}, f32[512,512]{1,0:T(8,128)S(1)}) custom-call(bf16[512,512]{1,0:T(8,128)(2,1)} %q_ref.7, bf16[512,512]{1,0:T(8,128)(2,1)} %k_ref.5, bf16[512,512]{1,0:T(8,128)(2,1)} %v_ref.5, bf16[512,512]{1,0:T(8,128)(2,1)} %copy-done.6, f32[512,128]{1,0:T(8,128)} %bitcast.12), custom_call_target="tpu_custom_call" | custom-call | flops 1140850688 | bytes 4980736 | tf_op jit(solution)/shard_map/backward_kernel/pallas_call | solution.py:42
  91.6 4.5 %all-to-all-done.4 = f32[64,9,1,128]{3,2,1,0:T(1,128)S(1)} async-done(((f32[64,9,1,128]{3,2,1,0:T(1,128)}), f32[64,9,1,128]{3,2,1,0:T(1,128)S(1)}, u32[]{:S(2)}, u32[]{:S(2)}) %all-to-all-start.4) | async-done | bytes 294944 | tf_op jit(solution)/shard_map/all_to_all | solution.py:219
  96.1 0.0 copy-done.1
  96.1 1.4 %final_kernel.1 = (bf16[512,512]{1,0:T(8,128)(2,1)}, bf16[512,512]{1,0:T(8,128)(2,1)}, f32[4,128]{1,0:T(4,128)}) custom-call(f32[512,512]{1,0:T(8,128)S(1)} %get-tuple-element.18.key_ref, f32[512,512]{1,0:T(8,128)S(1)} %get-tuple-element.19.value_ref, bf16[512,512]{1,0:T(8,128)(2,1)S(1)} %copy-done.1, bf16[512,512]{1,0:T(8,128)(2,1)S(1)} %copy-done.2, ...), custom_call_target="tpu_custom_call" | custom-call | flops 134217728 | bytes 4491264 | tf_op jit(solution)/shard_map/final_kernel/pallas_call | solution.py:42
  (5 shorter events, 0.0 us)
Async XLA Ops:
  28.7 18.6 %all-to-all-start.1 = ((f32[64,8,128]{2,1,0:T(8,128)}), f32[64,8,128]{2,1,0:T(8,128)S(1)}, u32[]{:S(2)}, u32[]{:S(2)}) async-start(f32[64,8,128]{2,1,0:T(8,128)} %prefix_kernel.1), calls=%async_computation.1 | async-start | bytes 524288 | tf_op jit(solution)/shard_map/all_to_all | solution.py:219
  38.5 8.9 %copy-start = (bf16[512,512]{1,0:T(8,128)(2,1)S(1)}, bf16[512,512]{1,0:T(8,128)(2,1)}, u32[]{:S(2)}) copy-start(bf16[512,512]{1,0:T(8,128)(2,1)} %q_ref.7) | copy-start | bytes 1572868
  38.5 8.9 %copy-start.3 = (bf16[512,512]{1,0:T(8,128)(2,1)S(1)}, bf16[512,512]{1,0:T(8,128)(2,1)}, u32[]{:S(2)}) copy-start(bf16[512,512]{1,0:T(8,128)(2,1)} %cot_ref.3) | copy-start | bytes 1572868
  41.4 6.0 %copy-start.5 = (f32[512]{0:T(512)S(1)}, f32[512]{0:T(512)}, u32[]{:S(2)}) copy-start(f32[512]{0:T(512)} %param.9) | copy-start | bytes 6148
  47.3 0.7 copy-start.4
  56.2 20.6 %copy-start.6 = (bf16[512,512]{1,0:T(8,128)(2,1)}, bf16[512,512]{1,0:T(8,128)(2,1)S(1)}, u32[]{:S(2)}) copy-start(bf16[512,512]{1,0:T(8,128)(2,1)S(1)} %get-tuple-element.16.grads_ref) | copy-start | bytes 1572868
  76.8 19.3 %all-to-all-start.4 = ((f32[64,9,1,128]{3,2,1,0:T(1,128)}), f32[64,9,1,128]{3,2,1,0:T(1,128)S(1)}, u32[]{:S(2)}, u32[]{:S(2)}) async-start(f32[64,9,1,128]{3,2,1,0:T(1,128)} %bitcast.5), calls=%async_computation.4 | async-start | bytes 589824 | tf_op jit(solution)/shard_map/all_to_all | solution.py:219
  86.5 9.5 %copy-start.1 = (bf16[512,512]{1,0:T(8,128)(2,1)S(1)}, bf16[512,512]{1,0:T(8,128)(2,1)}, u32[]{:S(2)}) copy-start(bf16[512,512]{1,0:T(8,128)(2,1)} %k_ref.5) | copy-start | bytes 1572868
  86.5 9.5 %copy-start.2 = (bf16[512,512]{1,0:T(8,128)(2,1)S(1)}, bf16[512,512]{1,0:T(8,128)(2,1)}, u32[]{:S(2)}) copy-start(bf16[512,512]{1,0:T(8,128)(2,1)} %v_ref.5) | copy-start | bytes 1572868
